TPU v7x, 128 devices: a whole 4x4x4 slice. The times are simulated.
128 devices in a mesh: side: 2 (over core), grp: 8 (over x_hi, y), tp: 8 (over x_lo, z).
Axes of the slice: x: 4 (x_hi: 2, x_lo: 2; x = x_hi * 2 + x_lo), y: 4, z: 4, core: 2. Of those that a mesh axis runs over, the one named last changes fastest.
Arguments:
- queries: bfloat16 [192, 4096], P('grp', 'side'), may hold values from -6 to 6
- kv_cache: bfloat16 [192, 16, 192, 256], P('grp', ('side', 'tp')), may hold values from -6 to 6
- lengths: int32 [192], P('grp'), may hold values from 2 to 768, as said below
- out_weight: bfloat16 [4096, 2048], P(('side', 'tp')), may hold values from -1 to 1
- resid: bfloat16 [192, 2048], P('grp'), may hold values from -6 to 6
- norm_gain: float32 [2048], replicated, may hold values from 0.1 to 1.9
- expert_ids: int32 [192, 8], P('grp'), may hold values from 0 to 127, all different within a row; in each aligned block of 24 rows (0 to 23, 24 to 47, ...) at most 3 rows name the same one
- expert_gates: float32 [192, 8], P('grp'), may hold values from 0.05 to 1
- w_gate_up: bfloat16 [128, 2048, 1536], P(('side', 'grp', 'tp')), may hold values from -0.125 to 0.125
- w_down: bfloat16 [128, 768, 2048], P(('side', 'grp', 'tp')), may hold values from -0.21875 to 0.21875
Outputs:
- layer_out: bfloat16 [192, 2048], P('grp', ('side', 'tp'))
Inputs may be any that keep to these rules, and one draw needn't show every extreme that they name: `lengths`: every row's cache holds at least two tokens; some row holds exactly 768. `expert_ids`: each row names 8 different experts. Among the rows of one row group no expert is named by more than 3 rows; in some group an expert is named by exactly 3.
All inputs are finite; a program needn't handle non-finite values.
Results may differ from a plain program's by a relative error of at most 0.017.
Values may be sent and summed in bfloat16 or wider, within the bound.
A program may use at most 64 MiB of HBM per device.

v0:
```python
import math
import jax
import jax.numpy as jnp
from jax import lax
from jax.sharding import PartitionSpec as P

QH = 32
KVH = 4
HD = 128
TOPK = 8


def swapped(value, axis, distance):
    mask = 2**distance
    pairs = [(source, source ^ mask) for source in range(lax.axis_size(axis))]
    return lax.ppermute(value, axis, pairs)


def body(
    queries,
    kv_cache,
    lengths,
    out_weight,
    resid,
    norm_gain,
    expert_ids,
    expert_gates,
    w_gate_up,
    w_down,
):
    lane_count = lax.axis_size("tp")
    tp_index = lax.axis_index("tp")
    side_count = lax.axis_size("side")
    section = lax.axis_index("side")
    grp_count = lax.axis_size("grp")
    group_size = side_count * lane_count
    member_index = section * lane_count + tp_index
    kv_parts = group_size // KVH
    group_heads = QH // KVH
    per_member = QH // group_size
    part_span = kv_cache.shape[2]
    model_width = out_weight.shape[1]
    piece_width = model_width // group_size
    rows_grp = lengths.shape[0]
    local_experts = w_gate_up.shape[0]
    experts_all = local_experts * side_count * grp_count * lane_count
    capacity = max(2, 2 * rows_grp * TOPK // experts_all)
    head_start = tp_index // kv_parts * group_heads * HD
    part_index = tp_index % kv_parts
    row_count = queries.shape[0]
    query_rows = lax.dynamic_slice_in_dim(queries, head_start, group_heads * HD, 1).reshape(
        row_count, group_heads, HD
    )
    key_rows = kv_cache[:, 0, :, :HD]
    value_rows = kv_cache[:, 0, :, HD:]
    positions = part_index * part_span + jnp.arange(part_span, dtype=jnp.int32)
    valid_mask = (positions[None, :] < lengths[:, None])[:, None, :]
    scores = jnp.einsum(
        "rgd,rpd->rgp", query_rows, key_rows, preferred_element_type=jnp.float32
    ) / math.sqrt(HD)
    scores = jnp.where(valid_mask, scores, -1e30)
    row_max = jnp.max(scores, axis=-1)
    for bit_index in range(kv_parts.bit_length() - 1):
        row_max = jnp.maximum(row_max, swapped(row_max, "tp", bit_index))
    weights = jnp.where(valid_mask, jnp.exp(scores - row_max[..., None]), 0.0)
    weight_sum = jnp.sum(weights, axis=-1)
    numerator = jnp.einsum(
        "rgp,rpd->rgd", weights.astype(jnp.bfloat16), value_rows, preferred_element_type=jnp.float32
    )
    for bit_index in range(kv_parts.bit_length() - 1):
        other_numerator, other_sum = swapped((numerator, weight_sum), "tp", bit_index)
        numerator = numerator + other_numerator
        weight_sum = weight_sum + other_sum
    heads_out = (numerator / weight_sum[..., None]).astype(jnp.bfloat16)
    mine = lax.dynamic_slice_in_dim(heads_out, part_index * per_member, per_member, 1).reshape(
        row_count, per_member * HD
    )
    projected = jnp.dot(mine, out_weight, preferred_element_type=jnp.float32)
    summed = lax.psum(projected, ("side", "tp"))
    middle = (resid.astype(jnp.float32) + summed).astype(jnp.bfloat16)
    middle_wide = middle.astype(jnp.float32)
    inv_rms = lax.rsqrt(jnp.mean(middle_wide * middle_wide, axis=-1, keepdims=True) + 1e-06)
    normed = (middle_wide * inv_rms * norm_gain).astype(jnp.bfloat16)
    column_experts = (
        (
            (section * grp_count + jnp.arange(grp_count, dtype=jnp.int32)[:, None]) * lane_count
            + tp_index
        )
        * local_experts
        + jnp.arange(local_experts, dtype=jnp.int32)[None, :]
    ).reshape(-1)
    matches = expert_ids[:, :, None] == column_experts[None, None, :]
    hit_count = jnp.sum(matches.astype(jnp.int32), axis=1)
    gate_cols = jnp.sum(jnp.where(matches, expert_gates[:, :, None], 0.0), axis=1)
    slot_rank = jnp.cumsum(hit_count, axis=0) - hit_count
    slot_ids = jnp.arange(capacity, dtype=jnp.int32)
    placed = (hit_count[:, :, None] == 1) & (slot_rank[:, :, None] == slot_ids[None, None, :])
    send_map = placed.astype(jnp.bfloat16)
    outgoing = jnp.einsum(
        "rcs,rd->csd", send_map, normed, preferred_element_type=jnp.float32
    ).astype(jnp.bfloat16)
    outgoing = outgoing.reshape(grp_count, local_experts, capacity, model_width)
    hidden = jnp.einsum(
        "gjcd,jdf->gjcf",
        lax.all_to_all(outgoing, "grp", split_axis=0, concat_axis=0, tiled=True),
        w_gate_up,
        preferred_element_type=jnp.float32,
    )
    inner_width = hidden.shape[-1] // 2
    activated = (jax.nn.silu(hidden[..., :inner_width]) * hidden[..., inner_width:]).astype(
        jnp.bfloat16
    )
    produced = jnp.einsum(
        "gjcf,jfd->gjcd", activated, w_down, preferred_element_type=jnp.float32
    ).astype(jnp.bfloat16)
    returned = lax.all_to_all(produced, "grp", split_axis=0, concat_axis=0, tiled=True)
    combine_weights = (send_map.astype(jnp.float32) * gate_cols[:, :, None]).reshape(row_count, -1)
    moe_part = jnp.dot(
        combine_weights,
        returned.reshape(-1, model_width).astype(jnp.float32),
        precision=lax.Precision.HIGHEST,
    )
    middle_mine = lax.dynamic_slice_in_dim(middle_wide, member_index * piece_width, piece_width, 1)
    moe_whole = lax.psum(moe_part, ("side", "tp"))
    return (
        middle_mine
        + lax.dynamic_slice_in_dim(moe_whole, member_index * piece_width, piece_width, 1)
    ).astype(jnp.bfloat16)


def solution(mesh):
    in_specs = (
        P("grp", "side"),
        P("grp", ("side", "tp"), None, None),
        P("grp"),
        P(("side", "tp"), None),
        P("grp", None),
        P(),
        P("grp", None),
        P("grp", None),
        P(("side", "grp", "tp"), None, None),
        P(("side", "grp", "tp"), None, None),
    )
    out_specs = P("grp", ("side", "tp"))
    return jax.shard_map(body, mesh=mesh, in_specs=in_specs, out_specs=out_specs, check_vma=False)
```

profile of v0, /device:TPU:1, one launch (start us, length us, event | category | flops | bytes accessed | tf_op | source)
XLA Modules:
  0.0 333.3 jit_solution(7118665528007655057)
XLA Ops:
  6.5 0.0 copy-start
  6.5 0.0 copy-start.3
  6.5 0.0 all-reduce.3.cloned.1.call-start
  6.6 1.0 dynamic-slice_bitcast_fusion
  7.5 0.7 broadcast_compare_fusion
  8.3 0.0 copy-start.1
  8.3 2.1 fusion.47
  10.3 2.5 collective-permute-start
  12.8 0.8 fusion.34
  13.6 0.3 collective-permute-done
  13.9 3.4 %collective-permute-start.1 = (f32[24,8]{1,0:T(8,128)S(1)}, f32[24,8]{1,0:T(8,128)S(1)}, u32[]{:S(2)}, u32[]{:S(2)}) collective-permute-start(f32[24,8]{1,0:T(8,128)S(1)} %max.6), channel_id=1, source_target_pairs={{0,2},{1,3},{2,0},{3,1},{4,6},{5,7},{6,4},{7,5},{8,10},{9,11},{10,... | collective-permute-start | bytes 2312 | tf_op jit(solution)/shard_map/ppermute | solution.py:16
  17.3 0.6 broadcast_compare_fusion.1
  17.9 0.6 collective-permute-done.1
  18.5 0.2 fusion.18
  18.7 1.0 collective-permute-start.4
  19.7 1.7 fusion.14
  21.4 0.5 collective-permute-start.2
  22.0 0.0 collective-permute-done.4
  22.0 2.9 collective-permute-start.5
  24.9 0.0 copy-done.3
  24.9 0.8 fusion.35
  25.7 0.1 copy.37
  25.8 0.1 copy.39
  25.9 1.1 collective-permute-done.5
  27.0 0.0 collective-permute-done.2
  27.0 2.0 collective-permute-start.3
  29.1 0.1 constant_dynamic-slice_fusion
  29.1 2.9 collective-permute-done.3
  32.1 0.1 fusion.37
  32.2 2.2 fusion.39
  34.4 0.0 all-reduce.3.cloned.1.call-update
  34.4 1.3 convert_multiply_fusion
  35.7 130.8 %all-reduce.3.cloned.1.call-done = f32[24,2048]{1,0:T(8,128)} async-done(((f32[24,2048]{1,0:T(8,128)}), f32[24,2048]{1,0:T(8,128)}) %all-reduce.3.cloned.1.call-update) | async-done | bytes 196624 | tf_op jit(solution)/shard_map/psum | solution.py:79
  166.5 0.0 copy-done.1
  166.5 1.1 multiply_reduce_fusion
  167.5 0.9 fusion.10
  168.5 0.1 copy.41
  168.6 13.4 %all_to_all.10 = bf16[8,1,3,2048]{3,2,1,0:T(4,128)(2,1)S(1)} all-to-all(bf16[8,1,3,2048]{3,2,1,0:T(4,128)(2,1)S(1)} %copy.41), channel_id=1, replica_groups=mesh['side'=2,'grp'=8,'tp'=8] {'grp'}, dimensions={0} | all-to-all | bytes 196608 | tf_op jit(solution)/shard_map/all_to_all | solution.py:105
  182.0 3.7 %fusion.4 = f32[8,1,3,1536]{3,0,2,1:T(8,128)S(1)} fusion(bf16[1,2048,1536]{2,1,0:T(8,128)(2,1)} %param.18, bf16[8,1,3,2048]{3,2,1,0:T(4,128)(2,1)S(1)} %all_to_all.10), kind=kOutput, calls=%fused_computation.4 | convolution fusion | flops 150994944 | bytes 6537216 | tf_op jit(solution)/shard_map/gjcd,jdf->gjcf/dot_general | solution.py:103
  185.7 0.0 copy-done
  185.7 0.0 copy-start.2
  185.7 0.5 fusion.11
  186.2 0.7 copy.43
  187.0 3.4 %all-to-all-start.1 = ((bf16[8,1,3,2048]{3,2,1,0:T(4,128)(2,1)}), bf16[8,1,3,2048]{3,2,1,0:T(4,128)(2,1)S(1)}, u32[]{:S(2)}, u32[]{:S(2)}) async-start(bf16[8,1,3,2048]{3,2,1,0:T(4,128)(2,1)} %copy.43), calls=%async_computation.1 | async-start | bytes 262144 | tf_op jit(solution)/shard_map/all_to_all | solution.py:116
  190.3 0.0 all-reduce.5.cloned.1.call-start
  190.4 0.0 copy-done.2
  190.4 6.8 %all-to-all-done.1 = bf16[8,1,3,2048]{3,2,1,0:T(4,128)(2,1)S(1)} async-done(((bf16[8,1,3,2048]{3,2,1,0:T(4,128)(2,1)}), bf16[8,1,3,2048]{3,2,1,0:T(4,128)(2,1)S(1)}, u32[]{:S(2)}, u32[]{:S(2)}) %all-to-all-start.1) | async-done | bytes 98336 | tf_op jit(solution)/shard_map/all_to_all | solution.py:116
  197.2 0.7 reshape.139
  197.9 1.9 fusion.48
  199.8 0.0 all-reduce.5.cloned.1.call-update
  199.8 125.3 %all-reduce.5.cloned.1.call-done = f32[24,2048]{1,0:T(8,128)} async-done(((f32[24,2048]{1,0:T(8,128)}), f32[24,2048]{1,0:T(8,128)}) %all-reduce.5.cloned.1.call-update) | async-done | bytes 196624 | tf_op jit(solution)/shard_map/psum | solution.py:124
  325.1 1.3 add_convert_fusion.1
  (12 shorter events, 0.1 us)
Async XLA Ops:
  6.5 179.2 %copy-start = (bf16[1,768,2048]{2,1,0:T(8,128)(2,1)S(1)}, bf16[1,768,2048]{2,1,0:T(8,128)(2,1)}, u32[]{:S(2)}) copy-start(bf16[1,768,2048]{2,1,0:T(8,128)(2,1)} %param.19) | copy-start | bytes 9437188
  6.5 18.4 %copy-start.3 = (s32[24,8]{0,1:T(8,128)S(1)}, s32[24,8]{0,1:T(8,128)}, u32[]{:S(2)}) copy-start(s32[24,8]{0,1:T(8,128)} %param.16) | copy-start | bytes 2308
  6.5 159.9 %all-reduce.3.cloned.1.call-start = ((), (), s32[]{:S(2)}) async-start(), calls=%async_computation.2 | async-start | bytes 393216 | tf_op jit(solution)/shard_map/psum | solution.py:79
  8.3 158.2 %copy-start.1 = (bf16[24,2048]{1,0:T(8,128)(2,1)S(1)}, bf16[24,2048]{1,0:T(8,128)(2,1)}, u32[]{:S(2)}) copy-start(bf16[24,2048]{1,0:T(8,128)(2,1)} %param.14) | copy-start | bytes 294916
  10.3 3.6 %collective-permute-start = (f32[24,8]{1,0:T(8,128)S(1)}, f32[24,8]{1,0:T(8,128)S(1)}, u32[]{:S(2)}, u32[]{:S(2)}) collective-permute-start(f32[24,8]{1,0:T(8,128)S(1)} %get-tuple-element.9), channel_id=1, source_target_pairs={{0,1},{1,0},{2,3},{3,2},{4,5},{5,4},{6,7},{7,6},{8,9},{9,8},{10,11... | collective-permute-start | bytes 2312 | tf_op jit(solution)/shard_map/ppermute | solution.py:16
  13.9 4.6 %collective-permute-start.1 = (f32[24,8]{1,0:T(8,128)S(1)}, f32[24,8]{1,0:T(8,128)S(1)}, u32[]{:S(2)}, u32[]{:S(2)}) collective-permute-start(f32[24,8]{1,0:T(8,128)S(1)} %max.6), channel_id=1, source_target_pairs={{0,2},{1,3},{2,0},{3,1},{4,6},{5,7},{6,4},{7,5},{8,10},{9,11},{10,... | collective-permute-start | bytes 2312 | tf_op jit(solution)/shard_map/ppermute | solution.py:16
  18.7 3.3 collective-permute-start.4
  21.4 5.6 %collective-permute-start.2 = (f32[24,8,128]{2,1,0:T(8,128)S(1)}, f32[24,8,128]{2,1,0:T(8,128)S(1)}, u32[]{:S(2)}, u32[]{:S(2)}) collective-permute-start(f32[24,8,128]{2,1,0:T(8,128)S(1)} %fusion.14), channel_id=1, source_target_pairs={{0,1},{1,0},{2,3},{3,2},{4,5},{5,4},{6,7},{7,6},{8,9},{9,8},{10,11... | collective-permute-start | bytes 294920 | tf_op jit(solution)/shard_map/ppermute | solution.py:16
  22.0 5.0 %collective-permute-start.5 = (f32[24,8]{1,0:T(8,128)S(1)}, f32[24,8]{1,0:T(8,128)S(1)}, u32[]{:S(2)}, u32[]{:S(2)}) collective-permute-start(f32[24,8]{1,0:T(8,128)S(1)} %add.92), channel_id=1, source_target_pairs={{0,2},{1,3},{2,0},{3,1},{4,6},{5,7},{6,4},{7,5},{8,10},{9,11},{10,... | collective-permute-start | bytes 2312 | tf_op jit(solution)/shard_map/ppermute | solution.py:16
  27.0 5.1 %collective-permute-start.3 = (f32[24,8,128]{2,1,0:T(8,128)S(1)}, f32[24,8,128]{2,1,0:T(8,128)S(1)}, u32[]{:S(2)}, u32[]{:S(2)}) collective-permute-start(f32[24,8,128]{2,1,0:T(8,128)S(1)} %add.90), channel_id=1, source_target_pairs={{0,2},{1,3},{2,0},{3,1},{4,6},{5,7},{6,4},{7,5},{8,10},{9,11},{10,... | collective-permute-start | bytes 294920 | tf_op jit(solution)/shard_map/ppermute | solution.py:16
  185.7 4.7 %copy-start.2 = (f32[24,8,3]{0,2,1:T(4,128)S(1)}, f32[24,8,3]{0,2,1:T(4,128)}, u32[]{:S(2)}) copy-start(f32[24,8,3]{0,2,1:T(4,128)} %get-tuple-element.7) | copy-start | bytes 6916
  187.0 10.3 %all-to-all-start.1 = ((bf16[8,1,3,2048]{3,2,1,0:T(4,128)(2,1)}), bf16[8,1,3,2048]{3,2,1,0:T(4,128)(2,1)S(1)}, u32[]{:S(2)}, u32[]{:S(2)}) async-start(bf16[8,1,3,2048]{3,2,1,0:T(4,128)(2,1)} %copy.43), calls=%async_computation.1 | async-start | bytes 262144 | tf_op jit(solution)/shard_map/all_to_all | solution.py:116
  190.3 134.8 %all-reduce.5.cloned.1.call-start = ((), (), s32[]{:S(2)}) async-start(), calls=%async_computation.3 | async-start | bytes 393216 | tf_op jit(solution)/shard_map/psum | solution.py:124
Sparse Core Ops, SparseCore 0:
  34.5 131.9 all-reduce.2
  199.9 125.1 all-reduce.4
where the time goes:
time: 334 us; the launch traced here: 333 us
  waiting for transfers between devices  268 us (80%)
  starting transfers between devices  15.9 us (5%)
  between operations  13.5 us (4%)
  blocking collectives  13.4 us (4%)
  matrix products  13 us (4%)
  other arithmetic  6.89 us (2%)
    psum x1, waiting for transfers between devices, body(): summed = lax.psum(projected, ('side', 'tp'))  131 us
    psum x1, waiting for transfers between devices, body(): moe_whole = lax.psum(moe_part, ('side', 'tp'))  125 us
    all_to_all x1, blocking collectives, body(): lax.all_to_all(outgoing, 'grp', split_axis=0, concat_axis=0, tiled=True)  13.4 us
    ppermute x6, starting transfers between devices, swapped(): return lax.ppermute(value, axis, pairs)  12.4 us
    all_to_all x1, waiting for transfers between devices, body(): lax.all_to_all(produced, 'grp', split_axis=0, concat_axis=0, tiled=True)  6.8 us
  transfers between devices with their start and end apart: 9, of which 7 were waited for; matrix products, arithmetic and copies ran while one was open for 2% of the time, Pallas kernels for 0%

commit v1 on v0

--- a/solution.py
+++ b/solution.py
@@ -76,7 +76,9 @@
         row_count, per_member * HD
     )
     projected = jnp.dot(mine, out_weight, preferred_element_type=jnp.float32)
-    summed = lax.psum(projected, ("side", "tp"))
+    summed = projected
+    for jj in ("side", "tp"):
+        summed = jax.lax.psum(summed, axis_name=jj)
     middle = (resid.astype(jnp.float32) + summed).astype(jnp.bfloat16)
     middle_wide = middle.astype(jnp.float32)
     inv_rms = lax.rsqrt(jnp.mean(middle_wide * middle_wide, axis=-1, keepdims=True) + 1e-06)

time: 334 us -> 307 us (0.919)
  waiting for transfers between devices: 268 us -> 244 us
    psum x1 -> x2, waiting for transfers between devices: 131 us -> 102 us  [body(): summed = jax.lax.psum(summed, axis_name=jj)]
    psum x1, waiting for transfers between devices: 125 us -> 129 us  [body(): moe_whole = lax.psum(moe_part, ('side', 'tp'))]
  transfers between devices with their start and end apart: 9 -> 10, of which waited for: 7 -> 8; matrix products, arithmetic and copies ran while one was open for 2% -> 1% of each run, Pallas kernels for 0% -> 0%
where the time goes in v1:
time: 307 us
  waiting for transfers between devices  244 us (79%)
  starting transfers between devices  15.9 us (5%)
  between operations  13.2 us (4%)
  matrix products  13 us (4%)
  blocking collectives  12.9 us (4%)
  other arithmetic  4.98 us (2%)
    psum x1, waiting for transfers between devices, body(): moe_whole = lax.psum(moe_part, ('side', 'tp'))  129 us
    psum x2, waiting for transfers between devices, body(): summed = jax.lax.psum(summed, axis_name=jj)  102 us
    all_to_all x1, blocking collectives, body(): lax.all_to_all(outgoing, 'grp', split_axis=0, concat_axis=0, tiled=True)  12.9 us
    ppermute x6, starting transfers between devices, swapped(): return lax.ppermute(value, axis, pairs)  12.4 us
    all_to_all x1, waiting for transfers between devices, body(): lax.all_to_all(produced, 'grp', split_axis=0, concat_axis=0, tiled=True)  6.8 us
    ppermute x6, waiting for transfers between devices, swapped(): return lax.ppermute(value, axis, pairs)  6.2 us
  transfers between devices with their start and end apart: 10, of which 8 were waited for; matrix products, arithmetic and copies ran while one was open for 1% of the time, Pallas kernels for 0%

profile of v1, /device:TPU:1, one launch (start us, length us, event | category | flops | bytes accessed | tf_op | source)
XLA Modules:
  0.0 306.9 jit_solution(7595563102747050186)
XLA Ops:
  6.5 0.0 copy-start
  6.5 0.0 copy-start.3
  6.5 0.0 all-reduce.4.cloned.1.call-start
  6.6 1.0 dynamic-slice_bitcast_fusion
  7.5 0.7 broadcast_compare_fusion
  8.3 2.1 fusion.47
  10.3 0.0 copy-start.1
  10.3 2.5 collective-permute-start
  12.8 1.1 collective-permute-done
  13.9 3.4 %collective-permute-start.1 = (f32[24,8]{1,0:T(8,128)S(1)}, f32[24,8]{1,0:T(8,128)S(1)}, u32[]{:S(2)}, u32[]{:S(2)}) collective-permute-start(f32[24,8]{1,0:T(8,128)S(1)} %max.6), channel_id=1, source_target_pairs={{0,2},{1,3},{2,0},{3,1},{4,6},{5,7},{6,4},{7,5},{8,10},{9,11},{10,... | collective-permute-start | bytes 2312 | tf_op jit(solution)/shard_map/ppermute | solution.py:16
  17.3 0.8 fusion.35
  18.1 0.4 collective-permute-done.1
  18.5 0.2 fusion.18
  18.7 1.0 collective-permute-start.4
  19.7 1.7 fusion.14
  21.4 0.5 collective-permute-start.2
  21.9 0.0 collective-permute-done.4
  22.0 2.9 collective-permute-start.5
  24.9 0.0 copy-done.3
  24.9 0.1 fusion.34
  25.0 0.1 copy.37
  25.1 0.1 copy.39
  25.2 1.8 collective-permute-done.5
  27.0 0.0 collective-permute-done.2
  27.0 2.0 collective-permute-start.3
  29.0 0.1 constant_dynamic-slice_fusion
  29.1 2.9 collective-permute-done.3
  32.1 0.1 fusion.37
  32.2 2.2 fusion.39
  34.3 0.0 all-reduce.4.cloned.1.call-update
  34.4 0.0 all-reduce.6.cloned.1.call-start
  34.4 30.1 %all-reduce.4.cloned.1.call-done = f32[24,2048]{1,0:T(8,128)} async-done(((f32[24,2048]{1,0:T(8,128)}), f32[24,2048]{1,0:T(8,128)}) %all-reduce.4.cloned.1.call-update) | async-done | bytes 196624 | tf_op jit(solution)/shard_map/psum | solution.py:81
  64.5 0.0 all-reduce.6.cloned.1.call-update
  64.6 0.6 convert_multiply_fusion
  65.2 71.6 %all-reduce.6.cloned.1.call-done = f32[24,2048]{1,0:T(8,128)} async-done(((f32[24,2048]{1,0:T(8,128)}), f32[24,2048]{1,0:T(8,128)}) %all-reduce.6.cloned.1.call-update) | async-done | bytes 196624 | tf_op jit(solution)/shard_map/psum | solution.py:81
  136.8 0.0 copy-done.1
  136.8 1.1 multiply_reduce_fusion
  137.9 0.9 fusion.10
  138.8 0.1 copy.41
  138.9 12.9 %all_to_all.10 = bf16[8,1,3,2048]{3,2,1,0:T(4,128)(2,1)S(1)} all-to-all(bf16[8,1,3,2048]{3,2,1,0:T(4,128)(2,1)S(1)} %copy.41), channel_id=1, replica_groups=mesh['side'=2,'grp'=8,'tp'=8] {'grp'}, dimensions={0} | all-to-all | bytes 196608 | tf_op jit(solution)/shard_map/all_to_all | solution.py:107
  151.8 3.7 %fusion.4 = f32[8,1,3,1536]{3,0,2,1:T(8,128)S(1)} fusion(bf16[1,2048,1536]{2,1,0:T(8,128)(2,1)} %param.18, bf16[8,1,3,2048]{3,2,1,0:T(4,128)(2,1)S(1)} %all_to_all.10), kind=kOutput, calls=%fused_computation.4 | convolution fusion | flops 150994944 | bytes 6537216 | tf_op jit(solution)/shard_map/gjcd,jdf->gjcf/dot_general | solution.py:105
  155.5 0.0 copy-done
  155.5 0.0 copy-start.2
  155.5 0.5 fusion.11
  156.1 0.7 copy.43
  156.8 3.4 %all-to-all-start.1 = ((bf16[8,1,3,2048]{3,2,1,0:T(4,128)(2,1)}), bf16[8,1,3,2048]{3,2,1,0:T(4,128)(2,1)S(1)}, u32[]{:S(2)}, u32[]{:S(2)}) async-start(bf16[8,1,3,2048]{3,2,1,0:T(4,128)(2,1)} %copy.43), calls=%async_computation.1 | async-start | bytes 262144 | tf_op jit(solution)/shard_map/all_to_all | solution.py:118
  160.2 0.0 all-reduce.8.cloned.1.call-start
  160.2 0.0 copy-done.2
  160.3 6.8 %all-to-all-done.1 = bf16[8,1,3,2048]{3,2,1,0:T(4,128)(2,1)S(1)} async-done(((bf16[8,1,3,2048]{3,2,1,0:T(4,128)(2,1)}), bf16[8,1,3,2048]{3,2,1,0:T(4,128)(2,1)S(1)}, u32[]{:S(2)}, u32[]{:S(2)}) %all-to-all-start.1) | async-done | bytes 98336 | tf_op jit(solution)/shard_map/all_to_all | solution.py:118
  167.1 0.7 reshape.139
  167.8 1.9 fusion.48
  169.6 0.0 all-reduce.8.cloned.1.call-update
  169.7 129.4 %all-reduce.8.cloned.1.call-done = f32[24,2048]{1,0:T(8,128)} async-done(((f32[24,2048]{1,0:T(8,128)}), f32[24,2048]{1,0:T(8,128)}) %all-reduce.8.cloned.1.call-update) | async-done | bytes 196624 | tf_op jit(solution)/shard_map/psum | solution.py:126
  299.1 1.3 add_convert_fusion.1
  (13 shorter events, 0.1 us)
Async XLA Ops:
  6.5 149.0 %copy-start = (bf16[1,768,2048]{2,1,0:T(8,128)(2,1)S(1)}, bf16[1,768,2048]{2,1,0:T(8,128)(2,1)}, u32[]{:S(2)}) copy-start(bf16[1,768,2048]{2,1,0:T(8,128)(2,1)} %param.19) | copy-start | bytes 9437188
  6.5 18.4 %copy-start.3 = (s32[24,8]{0,1:T(8,128)S(1)}, s32[24,8]{0,1:T(8,128)}, u32[]{:S(2)}) copy-start(s32[24,8]{0,1:T(8,128)} %param.16) | copy-start | bytes 2308
  6.5 58.0 %all-reduce.4.cloned.1.call-start = ((), (), s32[]{:S(2)}) async-start(), calls=%async_computation.2 | async-start | bytes 393216 | tf_op jit(solution)/shard_map/psum | solution.py:81
  10.3 126.5 %copy-start.1 = (bf16[24,2048]{1,0:T(8,128)(2,1)S(1)}, bf16[24,2048]{1,0:T(8,128)(2,1)}, u32[]{:S(2)}) copy-start(bf16[24,2048]{1,0:T(8,128)(2,1)} %param.14) | copy-start | bytes 294916
  10.3 3.6 %collective-permute-start = (f32[24,8]{1,0:T(8,128)S(1)}, f32[24,8]{1,0:T(8,128)S(1)}, u32[]{:S(2)}, u32[]{:S(2)}) collective-permute-start(f32[24,8]{1,0:T(8,128)S(1)} %get-tuple-element.9), channel_id=1, source_target_pairs={{0,1},{1,0},{2,3},{3,2},{4,5},{5,4},{6,7},{7,6},{8,9},{9,8},{10,11... | collective-permute-start | bytes 2312 | tf_op jit(solution)/shard_map/ppermute | solution.py:16
  13.9 4.6 %collective-permute-start.1 = (f32[24,8]{1,0:T(8,128)S(1)}, f32[24,8]{1,0:T(8,128)S(1)}, u32[]{:S(2)}, u32[]{:S(2)}) collective-permute-start(f32[24,8]{1,0:T(8,128)S(1)} %max.6), channel_id=1, source_target_pairs={{0,2},{1,3},{2,0},{3,1},{4,6},{5,7},{6,4},{7,5},{8,10},{9,11},{10,... | collective-permute-start | bytes 2312 | tf_op jit(solution)/shard_map/ppermute | solution.py:16
  18.7 3.3 %collective-permute-start.4 = (f32[24,8]{1,0:T(8,128)S(1)}, f32[24,8]{1,0:T(8,128)S(1)}, u32[]{:S(2)}, u32[]{:S(2)}) collective-permute-start(f32[24,8]{1,0:T(8,128)S(1)} %fusion.18), channel_id=1, source_target_pairs={{0,1},{1,0},{2,3},{3,2},{4,5},{5,4},{6,7},{7,6},{8,9},{9,8},{10,11... | collective-permute-start | bytes 2312 | tf_op jit(solution)/shard_map/ppermute | solution.py:16
  21.4 5.6 %collective-permute-start.2 = (f32[24,8,128]{2,1,0:T(8,128)S(1)}, f32[24,8,128]{2,1,0:T(8,128)S(1)}, u32[]{:S(2)}, u32[]{:S(2)}) collective-permute-start(f32[24,8,128]{2,1,0:T(8,128)S(1)} %fusion.14), channel_id=1, source_target_pairs={{0,1},{1,0},{2,3},{3,2},{4,5},{5,4},{6,7},{7,6},{8,9},{9,8},{10,11... | collective-permute-start | bytes 294920 | tf_op jit(solution)/shard_map/ppermute | solution.py:16
  22.0 5.0 %collective-permute-start.5 = (f32[24,8]{1,0:T(8,128)S(1)}, f32[24,8]{1,0:T(8,128)S(1)}, u32[]{:S(2)}, u32[]{:S(2)}) collective-permute-start(f32[24,8]{1,0:T(8,128)S(1)} %add.94), channel_id=1, source_target_pairs={{0,2},{1,3},{2,0},{3,1},{4,6},{5,7},{6,4},{7,5},{8,10},{9,11},{10,... | collective-permute-start | bytes 2312 | tf_op jit(solution)/shard_map/ppermute | solution.py:16
  27.0 5.1 %collective-permute-start.3 = (f32[24,8,128]{2,1,0:T(8,128)S(1)}, f32[24,8,128]{2,1,0:T(8,128)S(1)}, u32[]{:S(2)}, u32[]{:S(2)}) collective-permute-start(f32[24,8,128]{2,1,0:T(8,128)S(1)} %add.92), channel_id=1, source_target_pairs={{0,2},{1,3},{2,0},{3,1},{4,6},{5,7},{6,4},{7,5},{8,10},{9,11},{10,... | collective-permute-start | bytes 294920 | tf_op jit(solution)/shard_map/ppermute | solution.py:16
  34.4 102.5 %all-reduce.6.cloned.1.call-start = ((), (), s32[]{:S(2)}) async-start(), calls=%async_computation.3 | async-start | bytes 393216 | tf_op jit(solution)/shard_map/psum | solution.py:81
  155.5 4.7 %copy-start.2 = (f32[24,8,3]{0,2,1:T(4,128)S(1)}, f32[24,8,3]{0,2,1:T(4,128)}, u32[]{:S(2)}) copy-start(f32[24,8,3]{0,2,1:T(4,128)} %get-tuple-element.7) | copy-start | bytes 6916
  156.8 10.2 %all-to-all-start.1 = ((bf16[8,1,3,2048]{3,2,1,0:T(4,128)(2,1)}), bf16[8,1,3,2048]{3,2,1,0:T(4,128)(2,1)S(1)}, u32[]{:S(2)}, u32[]{:S(2)}) async-start(bf16[8,1,3,2048]{3,2,1,0:T(4,128)(2,1)} %copy.43), calls=%async_computation.1 | async-start | bytes 262144 | tf_op jit(solution)/shard_map/all_to_all | solution.py:118
  160.2 138.9 %all-reduce.8.cloned.1.call-start = ((), (), s32[]{:S(2)}) async-start(), calls=%async_computation.4 | async-start | bytes 393216 | tf_op jit(solution)/shard_map/psum | solution.py:126
Sparse Core Ops, SparseCore 0:
  34.5 30.0 all-reduce.3
  67.0 69.7 all-reduce.5
  169.8 129.2 all-reduce.7
